TPU v7x, 32 devices: a whole 2x2x4 slice. The times are simulated.
32 devices in a mesh: gx: 16 (over z, y, core), gy: 2 (over x).
Axes of the slice: x: 2, y: 2, z: 4, core: 2. Of those that a mesh axis runs over, the one named last changes fastest.
Arguments:
- velocity: float32 [3, 64, 32, 128], P(None, 'gx', 'gy'), may hold values from -3 to 3
- cauchy_green: float32 [6, 64, 32, 128], P(None, 'gx', 'gy'), may hold values from -0.25 to 1.5, as said below
- labels: int32 [64, 32, 128], P('gx', 'gy'), may hold values from 0 to 4
Outputs:
- new_velocity: float32 [3, 64, 32, 128], P(None, 'gx', 'gy')
- new_cauchy_green: float32 [6, 64, 32, 128], P(None, 'gx', 'gy')
- new_fraction: float32 [64, 32, 128], P('gx', 'gy')
Inputs may be any that keep to these rules, and one draw needn't show every extreme that they name: `cauchy_green`: the six components are xx, yy, zz, xy, xz, yz of a symmetric tensor; the three diagonal ones lie in 0.6 to 1.5 and the off-diagonal ones in -0.25 to 0.25.
All inputs are finite; a program needn't handle non-finite values.
Results may differ from a plain program's by a relative error of at most 0.0003.
Values sent between devices are 32-bit elements; how exact they have to be, the bound alone decides.
A program may use at most 64 MiB of HBM per device.

v0:
```python
import functools
import math

import jax
import jax.numpy as jnp
import numpy as np
from jax import lax
from jax.experimental import pallas as pl
from jax.experimental.pallas import tpu as pltpu
from jax.sharding import PartitionSpec as P

time_step = 0.1
shear_modulus = 4.0
dilation = 0.5
weno_eps = 1e-06
pair_list = ((0, 0), (1, 1), (2, 2), (0, 1), (0, 2), (1, 2))
slot_table = ((0, 3, 4), (3, 1, 5), (4, 5, 2))


def padded_2(block, sides, width):
    for axis, dim in sides:
        count = lax.axis_size(axis)
        forward = [(i, i + 1) for i in range(count - 1)]
        forward.append((count - 1, 0))
        backward = [(target, source) for source, target in forward]
        low = lax.ppermute(
            lax.slice_in_dim(block, block.shape[dim] - width, None, axis=dim), axis, forward
        )
        high = lax.ppermute(lax.slice_in_dim(block, 0, width, axis=dim), axis, backward)
        block = jnp.concatenate([low, block, high], axis=dim)
    return block


def weno_face(minus_two, minus_one, center, plus_one, plus_two):
    poly_zero = (2.0 * minus_two - 7.0 * minus_one + 11.0 * center) / 6.0
    poly_one = (-minus_one + 5.0 * center + 2.0 * plus_one) / 6.0
    poly_two = (2.0 * center + 5.0 * plus_one - plus_two) / 6.0
    curve_zero = minus_two - 2.0 * minus_one + center
    slope_zero = minus_two - 4.0 * minus_one + 3.0 * center
    curve_one = minus_one - 2.0 * center + plus_one
    slope_one = minus_one - plus_one
    curve_two = center - 2.0 * plus_one + plus_two
    slope_two = 3.0 * center - 4.0 * plus_one + plus_two
    smooth_zero = weno_eps + 13.0 / 12.0 * curve_zero * curve_zero + 0.25 * slope_zero * slope_zero
    smooth_one = weno_eps + 13.0 / 12.0 * curve_one * curve_one + 0.25 * slope_one * slope_one
    smooth_two = weno_eps + 13.0 / 12.0 * curve_two * curve_two + 0.25 * slope_two * slope_two
    weight_zero = 0.1 / (smooth_zero * smooth_zero)
    weight_one = 0.6 / (smooth_one * smooth_one)
    weight_two = 0.3 / (smooth_two * smooth_two)
    return (weight_zero * poly_zero + weight_one * poly_one + weight_two * poly_two) / (
        weight_zero + weight_one + weight_two
    )


def face_flux(shifted, speed_face):
    upwind_left = weno_face(shifted(-2), shifted(-1), shifted(0), shifted(1), shifted(2))
    upwind_right = weno_face(shifted(3), shifted(2), shifted(1), shifted(0), shifted(-1))
    return speed_face * jnp.where(speed_face >= 0.0, upwind_left, upwind_right)


def sweep(quantity, advecting, sweep_dim, anchor, count):

    def shifted(offset):
        return lax.slice_in_dim(
            quantity, anchor - 1 + offset, anchor + offset + count, axis=sweep_dim
        )

    speed_face = 0.5 * (
        lax.slice_in_dim(advecting, anchor - 1, anchor + count, axis=sweep_dim - 1)
        + lax.slice_in_dim(advecting, anchor, anchor + count + 1, axis=sweep_dim - 1)
    )
    flux_face = face_flux(shifted, speed_face)
    flux_upper = lax.slice_in_dim(flux_face, 1, count + 1, axis=sweep_dim)
    flux_lower = lax.slice_in_dim(flux_face, 0, count, axis=sweep_dim)
    center = lax.slice_in_dim(quantity, anchor, anchor + count, axis=sweep_dim)
    spread = lax.slice_in_dim(speed_face, 1, count + 1, axis=sweep_dim - 1) - lax.slice_in_dim(
        speed_face, 0, count, axis=sweep_dim - 1
    )
    return center * spread - (flux_upper - flux_lower)


def sweep_periodic(quantity, advecting):

    def shifted(offset):
        return jnp.roll(quantity, -offset, 3)

    speed_face = 0.5 * (advecting + jnp.roll(advecting, -1, 2))
    flux_face = face_flux(shifted, speed_face)
    return quantity * (speed_face - jnp.roll(speed_face, 1, 2)) - (
        flux_face - jnp.roll(flux_face, 1, 3)
    )


def region_gradient(padded, anchor, count_x, count_y):
    gradient = []
    for component in range(3):
        advecting = padded[7 + component]
        center = advecting[anchor : anchor + count_x, anchor : anchor + count_y]
        along_x = 0.5 * (
            advecting[anchor + 1 : anchor + 1 + count_x, anchor : anchor + count_y]
            - advecting[anchor - 1 : anchor - 1 + count_x, anchor : anchor + count_y]
        )
        along_y = 0.5 * (
            advecting[anchor : anchor + count_x, anchor + 1 : anchor + 1 + count_y]
            - advecting[anchor : anchor + count_x, anchor - 1 : anchor - 1 + count_y]
        )
        along_z = 0.5 * (jnp.roll(center, -1, 2) - jnp.roll(center, 1, 2))
        gradient.append([along_x, along_y, along_z])
    return gradient


def advance(green, fraction, transported, gradient):
    updated = []
    for component in range(6):
        left_index, right_index = pair_list[component]
        stretch = jnp.zeros_like(green[0])
        for inner_index in range(3):
            stretch = (
                stretch
                + gradient[left_index][inner_index] * green[slot_table[inner_index][right_index]]
            )
            stretch = (
                stretch
                + green[slot_table[left_index][inner_index]] * gradient[right_index][inner_index]
            )
        updated.append(green[component] + time_step * (transported[component] + stretch))
    return (jnp.stack(updated), fraction + time_step * transported[6])


def membrane_stress(green, fraction):
    determinant = (
        green[0] * (green[1] * green[2] - green[5] * green[5])
        - green[3] * (green[3] * green[2] - green[5] * green[4])
        + green[4] * (green[3] * green[5] - green[1] * green[4])
    )
    dilate = dilation * (determinant - 1.0)
    stress_parts = []
    for component in range(6):
        if component < 3:
            stress_parts.append(green[component] - 1.0 + dilate)
        else:
            stress_parts.append(green[component])
    return shear_modulus * fraction * jnp.stack(stress_parts)


def update_region(padded, anchor, count_x, count_y):
    carried = padded[:7]
    transported = sweep(
        carried[:, :, anchor : anchor + count_y],
        padded[7, :, anchor : anchor + count_y],
        1,
        anchor,
        count_x,
    )
    transported = transported + sweep(
        carried[:, anchor : anchor + count_x],
        padded[8, anchor : anchor + count_x],
        2,
        anchor,
        count_y,
    )
    region = padded[:, anchor : anchor + count_x, anchor : anchor + count_y]
    transported = transported + sweep_periodic(region[:7], region[9])
    gradient = region_gradient(padded, anchor, count_x, count_y)
    new_green, new_fraction = advance(region[:6], region[6], transported, gradient)
    return (new_green, new_fraction, membrane_stress(new_green, new_fraction))


def derive_x(widened):
    return 0.5 * (widened[..., 2:, 1:-1, :] - widened[..., :-2, 1:-1, :])


def derive_y(widened):
    return 0.5 * (widened[..., 1:-1, 2:, :] - widened[..., 1:-1, :-2, :])


def derive_z(widened):
    inside = widened[..., 1:-1, 1:-1, :]
    return 0.5 * (jnp.roll(inside, -1, -1) - jnp.roll(inside, 1, -1))


def stress_force(widened):
    return jnp.stack(
        [
            derive_x(widened[slot_table[index_row][0]])
            + derive_y(widened[slot_table[index_row][1]])
            + derive_z(widened[slot_table[index_row][2]])
            for index_row in range(3)
        ]
    )


def dft_tables(length):
    wave_index = jnp.arange(length, dtype=jnp.int32)
    phase_index = wave_index[:, None] * wave_index[None, :] % length
    angle_table = 2.0 * math.pi / length * phase_index.astype(jnp.float32)
    return (jnp.cos(angle_table), jnp.sin(angle_table))


def contract(einsum_form, values, dft_table):
    return jnp.einsum(einsum_form, values, dft_table, precision=lax.Precision.HIGHEST)


def forward_transform(cell_field):
    components, cells_x, cells_y, length_z = cell_field.shape
    length_x = cells_x * lax.axis_size("gx")
    length_y = cells_y * lax.axis_size("gy")
    slab_z = length_z // lax.axis_size("gx")
    cosine_z, sine_z = dft_tables(length_z)
    real_z = contract("cxyz,zk->cxyk", cell_field, cosine_z)
    imag_z = -contract("cxyz,zk->cxyk", cell_field, sine_z)
    lines_x = lax.all_to_all(
        jnp.stack([real_z, imag_z], 1), "gx", split_axis=4, concat_axis=2, tiled=True
    )
    lines_x = lines_x.reshape(components, 2, length_x, cells_y * slab_z)
    cosine_x, sine_x = dft_tables(length_x)
    real_part = lines_x[:, 0]
    imag_part = lines_x[:, 1]
    real_x = contract("cxm,xk->ckm", real_part, cosine_x) + contract(
        "cxm,xk->ckm", imag_part, sine_x
    )
    imag_x = contract("cxm,xk->ckm", imag_part, cosine_x) - contract(
        "cxm,xk->ckm", real_part, sine_x
    )
    paired_x = jnp.stack([real_x, imag_x], 1).reshape(components, 2, length_x, cells_y, slab_z)
    lines_y = lax.all_to_all(paired_x, "gy", split_axis=2, concat_axis=3, tiled=True)
    cosine_y, sine_y = dft_tables(length_y)
    real_part = lines_y[:, 0]
    imag_part = lines_y[:, 1]
    real_y = contract("cayz,yk->ckaz", real_part, cosine_y) + contract(
        "cayz,yk->ckaz", imag_part, sine_y
    )
    imag_y = contract("cayz,yk->ckaz", imag_part, cosine_y) - contract(
        "cayz,yk->ckaz", real_part, sine_y
    )
    return (real_y, imag_y)


def inverse_transform(real_k, imag_k, cells_y, length_z):
    components, length_y, block_x, slab_z = real_k.shape
    length_x = block_x * lax.axis_size("gy")
    cosine_y, sine_y = dft_tables(length_y)
    real_y = contract("ckaz,ky->cayz", real_k, cosine_y) - contract("ckaz,ky->cayz", imag_k, sine_y)
    imag_y = contract("ckaz,ky->cayz", real_k, sine_y) + contract("ckaz,ky->cayz", imag_k, cosine_y)
    lines_x = lax.all_to_all(
        jnp.stack([real_y, imag_y], 1), "gy", split_axis=3, concat_axis=2, tiled=True
    )
    lines_x = lines_x.reshape(components, 2, length_x, cells_y * slab_z)
    cosine_x, sine_x = dft_tables(length_x)
    real_part = lines_x[:, 0]
    imag_part = lines_x[:, 1]
    real_x = contract("ckm,kx->cxm", real_part, cosine_x) - contract(
        "ckm,kx->cxm", imag_part, sine_x
    )
    imag_x = contract("ckm,kx->cxm", real_part, sine_x) + contract(
        "ckm,kx->cxm", imag_part, cosine_x
    )
    paired_x = jnp.stack([real_x, imag_x], 1).reshape(components, 2, length_x, cells_y, slab_z)
    slab_pairs = lax.all_to_all(paired_x, "gx", split_axis=2, concat_axis=4, tiled=True)
    cosine_z, sine_z = dft_tables(length_z)
    result = contract("cxyk,kz->cxyz", slab_pairs[:, 0], cosine_z) - contract(
        "cxyk,kz->cxyz", slab_pairs[:, 1], sine_z
    )
    return result / float(length_x * length_y * length_z)


def sine_numbers(wave_index, length):
    silent = wave_index % (length // 2) == 0
    sine_value = jnp.sin(2.0 * math.pi / length * wave_index.astype(jnp.float32))
    return (jnp.where(silent, 0.0, sine_value), silent)


def wave_numbers(length_y, block_x, slab_z, length_x, length_z):
    index_y = jnp.arange(length_y, dtype=jnp.int32)
    index_x = lax.axis_index("gy") * block_x + jnp.arange(block_x, dtype=jnp.int32)
    index_z = lax.axis_index("gx") * slab_z + jnp.arange(slab_z, dtype=jnp.int32)
    sine_x, silent_x = sine_numbers(index_x, length_x)
    sine_y, silent_y = sine_numbers(index_y, length_y)
    sine_z, silent_z = sine_numbers(index_z, length_z)
    live_mode = jnp.logical_not(
        silent_y[:, None, None] & silent_x[None, :, None] & silent_z[None, None, :]
    )
    return ((sine_x[None, :, None], sine_y[:, None, None], sine_z[None, None, :]), live_mode)


def local(velocity, cauchy_green, labels):
    cells_x = velocity.shape[1]
    cells_y = velocity.shape[2]
    length_z = velocity.shape[3]
    fraction = labels.astype(jnp.float32) * 0.25
    stacked = jnp.concatenate([cauchy_green, fraction[None], velocity], 0)
    padded = padded_2(stacked, (("gx", 1), ("gy", 2)), 4)
    green_wide, fraction_wide, stress_wide = update_region(padded, 3, cells_x + 2, cells_y + 2)
    new_green = green_wide[:, 1:-1, 1:-1]
    new_fraction = fraction_wide[1:-1, 1:-1]
    predicted = velocity + time_step * stress_force(stress_wide)
    length_x = cells_x * lax.axis_size("gx")
    velocity_wide = padded_2(predicted, (("gx", 1), ("gy", 2)), 1)
    divergence = (
        derive_x(velocity_wide[0]) + derive_y(velocity_wide[1]) + derive_z(velocity_wide[2])
    )
    real_k, imag_k = forward_transform(divergence[None])
    sine_list, live_mode = wave_numbers(
        real_k.shape[1], real_k.shape[2], real_k.shape[3], length_x, length_z
    )
    norm_sq = (
        sine_list[0] * sine_list[0] + sine_list[1] * sine_list[1] + sine_list[2] * sine_list[2]
    )
    safe_norm = jnp.where(live_mode, norm_sq, 1.0)
    pressure_real = jnp.where(live_mode, -real_k[0] / safe_norm, 0.0)
    pressure_imag = jnp.where(live_mode, -imag_k[0] / safe_norm, 0.0)
    pressure = inverse_transform(pressure_real[None], pressure_imag[None], cells_y, length_z)
    pressure_wide = padded_2(pressure, (("gx", 1), ("gy", 2)), 1)
    new_velocity = predicted - jnp.stack(
        [derive_x(pressure_wide[0]), derive_y(pressure_wide[0]), derive_z(pressure_wide[0])]
    )
    return (new_velocity, new_green, new_fraction)


def hartley(length):
    index = np.arange(length)
    angle = 2.0 * np.pi / length * (np.outer(index, index) % length)
    return np.cos(angle) + np.sin(angle)


def sine_squares(length):
    index = np.arange(length)
    sine = np.where(index % (length // 2) == 0, 0.0, np.sin(2.0 * np.pi / length * index))
    return sine * sine


def back_lanes(cells_x, cells_y):
    return -(-(cells_x + 2) * (cells_y + 2) // 128) * 128


def spectral_tables(count_x, count_y, cells_x, cells_y, length_z):
    length_x, length_y = count_x * cells_x, count_y * cells_y
    devices = count_x * count_y
    rows = length_z // devices
    table_x, table_y, table_z = hartley(length_x), hartley(length_y), hartley(length_z)
    wide = cells_x + 4
    stencils = (
        {0: 1.0},
        {-1: 0.5, 1: -0.5},
        {-2: 0.25, 0: -0.5, 2: 0.25},
    )
    field_orders = ((2, 0), (1, 1), (1, 0), (0, 2), (0, 1), (0, 0))
    send_table = np.zeros((count_y, 6, cells_x, cells_y, wide, length_y))
    near_x, near_y = cells_x + 2, cells_y + 2
    take_table = np.zeros((3, cells_x, cells_y, back_lanes(cells_x, cells_y)))
    turn_table = np.zeros((length_y, count_y, near_y))
    for block in range(count_y):
        place = block * cells_y + np.arange(cells_y)
        along = [
            sum(w * table_y[(place + o) % length_y] for o, w in stencil.items())
            for stencil in stencils
        ]
        for field, (order_x, order_y) in enumerate(field_orders):
            for cell in range(cells_x):
                for offset, weight in stencils[order_x].items():
                    send_table[block, field, cell, :, cell + 2 + offset] += weight * along[order_y]
        ring = (block * cells_y + np.arange(near_y) - 1) % length_y
        turn_table[:, block] = table_y[:, ring]
    for x in range(cells_x):
        for y in range(cells_y):
            place = (x + 1) * near_y + y + 1
            take_table[0, x, y, place + near_y] = 0.5
            take_table[0, x, y, place - near_y] = -0.5
            take_table[1, x, y, place + 1] = 0.5
            take_table[1, x, y, place - 1] = -0.5
            take_table[2, x, y, place] = 1.0
    same = np.eye(rows)
    reach = (
        np.arange(count_x)[None, :] * cells_x + np.arange(wide)[:, None] - 2
    ) % length_x
    solve_in = np.einsum("kib,qr->kqibr", table_x[:, reach], same).reshape(
        length_x * rows, wide * count_x * rows
    )
    home = np.arange(count_x)[None, :] * cells_x + np.arange(near_x)[:, None] - 1
    solve_out = np.einsum("ibk,qr->ibqkr", table_x[home % length_x], same).reshape(
        near_x * count_x * rows, length_x * rows
    )
    square_xy = np.repeat(sine_squares(length_x), rows)[:, None] + sine_squares(length_y)[None, :]
    square_z = sine_squares(length_z).reshape(devices, rows)
    square_z = np.tile(square_z, (1, 8 // rows))[:, :, None] * np.ones((1, 1, length_y))
    made = (
        table_z,
        send_table.reshape(count_y, 6 * cells_x * cells_y, wide * length_y),
        solve_in,
        solve_out,
        square_xy.reshape(-1, 8, length_y),
        square_z,
        take_table.reshape(3 * cells_x * cells_y, -1),
        turn_table.reshape(length_y, count_y * near_y),
    )
    return tuple(np.asarray(table, np.float32) for table in made)


def shift(values, offset, axis):
    extent = values.shape[axis]
    if offset % extent == 0:
        return values
    return pltpu.roll(values, (-offset) % extent, axis)


def weno_one(a, b, c, d, e):
    poly_zero = 2.0 * a - 7.0 * b + 11.0 * c
    poly_one = 5.0 * c - b + 2.0 * d
    poly_two = 2.0 * c + 5.0 * d - e
    curve_zero = a - 2.0 * b + c
    slope_zero = a - 4.0 * b + 3.0 * c
    curve_one = b - 2.0 * c + d
    slope_one = b - d
    curve_two = c - 2.0 * d + e
    slope_two = 3.0 * c - 4.0 * d + e
    big = 13.0 / 12.0
    smooth_zero = weno_eps + big * curve_zero * curve_zero + 0.25 * slope_zero * slope_zero
    smooth_one = weno_eps + big * curve_one * curve_one + 0.25 * slope_one * slope_one
    smooth_two = weno_eps + big * curve_two * curve_two + 0.25 * slope_two * slope_two
    zero_one = smooth_zero * smooth_one
    zero_two = smooth_zero * smooth_two
    one_two = smooth_one * smooth_two
    weight_zero = one_two * one_two
    weight_one = 6.0 * (zero_two * zero_two)
    weight_two = 3.0 * (zero_one * zero_one)
    return (weight_zero * poly_zero + weight_one * poly_one + weight_two * poly_two) / (
        6.0 * (weight_zero + weight_one + weight_two)
    )


def upwind_flux(at, speed):
    positive = speed >= 0.0
    minus_two, minus_one, center, one, two, three = [at(o) for o in range(-2, 4)]
    pick = functools.partial(jnp.where, positive)
    return speed * weno_one(
        pick(minus_two, three),
        pick(minus_one, two),
        pick(center, one),
        pick(one, center),
        pick(two, minus_one),
    )


def ring_sweep(values, advecting, axis):
    speed = 0.5 * (advecting + shift(advecting, 1, axis))
    flux = upwind_flux(lambda o: shift(values, o, axis), speed)
    return values * (speed - shift(speed, -1, axis)) - (flux - shift(flux, -1, axis))


def exact_dot(left, right, dims=((1,), (0,))):
    return lax.dot_general(
        left,
        right,
        (dims, ((), ())),
        precision=lax.Precision.HIGHEST,
        preferred_element_type=jnp.float32,
    )


def step_kernel(
    count_x,
    count_y,
    vel_far,
    green_far,
    labels_far,
    table_z_far,
    send_table_far,
    solve_in_far,
    solve_out_far,
    square_xy_far,
    square_z_far,
    take_table_far,
    turn_table_far,
    out_vel,
    out_green,
    out_frac,
    final,
    table_z,
    take_table,
    vel,
    green,
    labels,
    send_table,
    solve_in,
    solve_out,
    square_xy,
    square_z,
    turn_table,
    field,
    moved,
    pack,
    vel_pack,
    low_green,
    high_green,
    low_label,
    high_label,
    low_vel,
    high_vel,
    side,
    vel_near,
    vel_side,
    stress,
    stress_pack,
    stress_low,
    stress_high,
    stress_side,
    outbox,
    inbox,
    lines,
    backbox,
    homebox,
    load_sem,
    halo_sem,
    stress_sem,
    go_send,
    go_recv,
    back_send,
    back_recv,
    own_sem,
):
    cells_x, cells_y, length_z = labels.shape
    devices = count_x * count_y
    rows = length_z // devices
    length_y = count_y * cells_y
    wide = cells_x + 4
    me_x = lax.axis_index("gx")
    me_y = lax.axis_index("gy")
    me = me_x * count_y + me_y
    mesh_type = pl.DeviceIdType.MESH

    turns = []
    for bit in range(count_x.bit_length() - 1):
        weight = 1 << bit
        turns.append(weight * (1 - 2 * lax.rem(me_x // weight, 2)))
    others = []
    for step in range(devices - 1, 0, -1):
        peer_x, peer_y = me_x, me_y
        for bit, turn in enumerate(turns):
            if (step // count_y) >> bit & 1:
                peer_x = peer_x + turn
        if step % count_y:
            peer_y = 1 - me_y
        others.append((peer_x * count_y + peer_y, (peer_x, peer_y)))

    barrier = pltpu.get_barrier_semaphore()
    for _, device in others:
        pl.semaphore_signal(barrier, inc=1, device_id=device, device_id_type=mesh_type)

    load_list = (
        (vel_far, vel),
        (green_far, green),
        (labels_far, labels),
        (table_z_far, table_z),
        (send_table_far.at[me_y], send_table),
        (square_xy_far, square_xy),
        (square_z_far.at[me], square_z),
        (solve_in_far, solve_in),
        (solve_out_far, solve_out),
        (take_table_far, take_table),
        (turn_table_far, turn_table),
    )
    loads = [
        pltpu.make_async_copy(source, target, load_sem.at[n])
        for n, (source, target) in enumerate(load_list)
    ]
    for copy in loads:
        copy.start()
    for copy in loads[:3]:
        copy.wait()

    fraction = labels[...].astype(jnp.float32) * 0.25
    for c in range(6):
        field[c] = green[c]
    field[6] = fraction
    row = lax.broadcasted_iota(jnp.int32, (cells_x, 8, length_z), 1)

    def fold(values):
        return jnp.where(row < 4, values[:, :8], values[:, cells_y - 8 :])

    for c in range(7):
        pack[c] = fold(field[c])
    for c in range(3):
        for x in range(cells_x):
            vel_pack[c, 2 * x] = vel[c, x, 0]
            vel_pack[c, 2 * x + 1] = vel[c, x, cells_y - 1]
            vel_side[c, x] = jnp.zeros((8, length_z), jnp.float32)

    pl.semaphore_wait(barrier, devices - 1)

    right = (lax.rem(me_x + 1, count_x), me_y)
    left = (lax.rem(me_x + count_x - 1, count_x), me_y)
    over = (me_x, lax.rem(me_y + 1, count_y))

    def remote(source, target, send_sem, recv_sem, device):
        return pltpu.make_async_remote_copy(
            src_ref=source,
            dst_ref=target,
            send_sem=send_sem,
            recv_sem=recv_sem,
            device_id=device,
            device_id_type=mesh_type,
        )

    halo_list = (
        (vel_pack, vel_near, over),
        (pack, side, over),
        (green.at[:, cells_x - 3 :], low_green, right),
        (green.at[:, :3], high_green, left),
        (vel.at[:, cells_x - 1 :], low_vel, right),
        (vel.at[:, :1], high_vel, left),
        (labels.at[cells_x - 3 :], low_label, right),
        (labels.at[:3], high_label, left),
    )
    halos = [
        remote(source, target, halo_sem.at[0, n], halo_sem.at[1, n], device)
        for n, (source, target, device) in enumerate(halo_list)
    ]
    for copy in halos:
        copy.start()

    def sweep_z(c, carry):
        for x in range(cells_x):
            moved[c, x] = ring_sweep(field[c, x], vel[2, x], 1)
        return carry

    lax.fori_loop(0, 7, sweep_z, 0)

    halos[0].wait()
    for c in range(3):
        for x in range(cells_x):
            vel_side[c, x, 0] = vel_near[c, 2 * x]
            vel_side[c, x, 7] = vel_near[c, 2 * x + 1]
    halos[1].wait()

    def sweep_y(c, carry):
        for x in range(cells_x):
            values = jnp.concatenate([field[c, x], side[c, x]], axis=0)
            advecting = jnp.concatenate([vel[1, x], vel_side[1, x]], axis=0)
            moved[c, x] = moved[c, x] + ring_sweep(values, advecting, 0)[:cells_y]
        return carry

    lax.fori_loop(0, 7, sweep_y, 0)

    for copy in halos[2:]:
        copy.wait()

    def wide_vel(c):
        return jnp.concatenate([low_vel[c], vel[c], high_vel[c]], axis=0)

    def sweep_x(values, c):
        advecting = [low_vel[0, 0]] + [vel[0, x] for x in range(cells_x)] + [high_vel[0, 0]]
        flux = []
        speeds = []
        for face in range(cells_x + 1):
            speed = 0.5 * (advecting[face] + advecting[face + 1])
            speeds.append(speed)
            flux.append(upwind_flux(lambda o: values[face + 2 + o], speed))
        for x in range(cells_x):
            moved[c, x] = (
                moved[c, x]
                + values[x + 3] * (speeds[x + 1] - speeds[x])
                - (flux[x + 1] - flux[x])
            )

    def sweep_green(c, carry):
        values = [low_green[c, n] for n in range(3)]
        values += [field[c, x] for x in range(cells_x)]
        values += [high_green[c, n] for n in range(3)]
        sweep_x(values, c)
        return carry

    lax.fori_loop(0, 6, sweep_green, 0)
    values = [low_label[n].astype(jnp.float32) * 0.25 for n in range(3)]
    values += [field[6, x] for x in range(cells_x)]
    values += [high_label[n].astype(jnp.float32) * 0.25 for n in range(3)]
    sweep_x(values, 6)

    def central_z(block):
        return 0.5 * (shift(block, 1, 2) - shift(block, -1, 2))

    def central_y(block, edge):
        ring = jnp.concatenate([block, edge], axis=1)
        return (0.5 * (shift(ring, 1, 1) - shift(ring, -1, 1)))[:, :cells_y]

    def central_x(ring):
        return 0.5 * (ring[2:] - ring[:-2])

    gradient = [
        [central_x(wide_vel(c)), central_y(vel[c], vel_side[c]), central_z(vel[c])]
        for c in range(3)
    ]
    old = [field[c] for c in range(6)]
    new = []
    for c in range(6):
        left_index, right_index = pair_list[c]
        stretch = None
        for inner in range(3):
            term = (
                gradient[left_index][inner] * old[slot_table[inner][right_index]]
                + old[slot_table[left_index][inner]] * gradient[right_index][inner]
            )
            stretch = term if stretch is None else stretch + term
        new.append(old[c] + time_step * (moved[c] + stretch))
        out_green[c] = new[c]
    new_fraction = field[6] + time_step * moved[6]
    out_frac[...] = new_fraction
    determinant = (
        new[0] * (new[1] * new[2] - new[5] * new[5])
        - new[3] * (new[3] * new[2] - new[5] * new[4])
        + new[4] * (new[3] * new[5] - new[1] * new[4])
    )
    dilate = dilation * (determinant - 1.0)
    scale = shear_modulus * new_fraction
    sigma = [scale * (new[c] - 1.0 + dilate) for c in range(3)]
    sigma += [scale * new[c] for c in range(3, 6)]
    xx, yy, zz, xy, xz, yz = sigma
    for n, part in enumerate((xx, xz, xy, yy, yz, zz)):
        stress[n] = part
    for n, part in enumerate((xy, yy, yz)):
        stress_pack[n] = fold(part)

    parts = (
        time_step * xx,
        2.0 * time_step * xy,
        vel[0] + 2.0 * time_step * central_z(xz),
        time_step * yy,
        vel[1] + 2.0 * time_step * central_z(yz),
        central_z(vel[2] + time_step * central_z(zz)),
    )
    stacked = jnp.concatenate(
        [part.reshape(cells_x * cells_y, length_z) for part in parts], axis=0
    )
    for copy in loads[3:]:
        copy.wait()
    modes_z = exact_dot(table_z[...], stacked, ((1,), (1,)))
    modes_zy = exact_dot(modes_z, send_table[...])
    for n in range(devices):
        outbox[n] = modes_zy[n * rows : (n + 1) * rows]

    for target, device in others:
        remote(outbox.at[target], inbox.at[me], go_send.at[target], go_recv.at[me], device).start()
    keep = pltpu.make_async_copy(outbox.at[me], inbox.at[me], own_sem.at[0])
    keep.start()
    stress_list = (
        (stress_pack, stress_side, over),
        (stress.at[:3, cells_x - 1 :], stress_low, right),
        (stress.at[:3, :1], stress_high, left),
    )
    edges = [
        remote(source, target, stress_sem.at[0, n], stress_sem.at[1, n], device)
        for n, (source, target, device) in enumerate(stress_list)
    ]
    for copy in edges:
        copy.start()

    norm = square_xy[...] + square_z[...][None]
    live = norm > 0.0
    total = float(count_x * cells_x * length_y * length_z)
    green_function = jnp.where(live, (-1.0 / total) / jnp.where(live, norm, 1.0), 0.0)
    green_function = green_function.reshape(-1, length_y)

    for source, device in reversed(others):
        remote(
            outbox.at[source], inbox.at[source], go_send.at[source], go_recv.at[source], device
        ).wait()
    keep.wait()

    for n in range(count_x):
        held = inbox[n * count_y]
        for m in range(1, count_y):
            held = held + inbox[n * count_y + m]
        lines[n * rows : (n + 1) * rows] = held
    arranged = jnp.concatenate(
        [lines[:, n * length_y : (n + 1) * length_y] for n in range(wide)], axis=0
    )
    pressure_modes = exact_dot(solve_in[...], arranged) * green_function
    pressure = exact_dot(solve_out[...], exact_dot(pressure_modes, turn_table[...]))
    height = count_x * rows
    near_y = cells_y + 2
    for m in range(count_y):
        spread = jnp.concatenate(
            [
                pressure[n * height : (n + 1) * height, m * near_y : (m + 1) * near_y]
                for n in range(cells_x + 2)
            ]
            + [jnp.zeros((height, backbox.shape[2] - (cells_x + 2) * near_y), jnp.float32)],
            axis=1,
        )
        for n in range(count_x):
            backbox[n * count_y + m] = spread[n * rows : (n + 1) * rows]

    for target, device in others:
        remote(
            backbox.at[target], homebox.at[me], back_send.at[target], back_recv.at[me], device
        ).start()
    stay = pltpu.make_async_copy(backbox.at[me], homebox.at[me], own_sem.at[1])
    stay.start()

    for copy in edges:
        copy.wait()
    force = (
        (0, 2, 0, 1),
        (2, 3, 1, 4),
        (1, 4, 2, 5),
    )
    for c, (part_x, part_y, edge_y, part_z) in enumerate(force):
        ring = jnp.concatenate([stress_low[part_x], stress[part_x], stress_high[part_x]], axis=0)
        pushed = (
            central_x(ring)
            + central_y(stress[part_y], stress_side[edge_y])
            + central_z(stress[part_z])
        )
        out_vel[c] = vel[c] + time_step * pushed

    for source, device in reversed(others):
        remote(
            backbox.at[source], homebox.at[source], back_send.at[source], back_recv.at[source], device
        ).wait()
    stay.wait()
    for n in range(devices):
        final[n * rows : (n + 1) * rows] = homebox[n]


def finish_kernel(
    predicted,
    green,
    fraction,
    final,
    table_z,
    take_table,
    out_vel,
    out_green,
    out_frac,
    vel,
    sems,
):
    store_green = pltpu.make_async_copy(green, out_green, sems.at[0])
    store_frac = pltpu.make_async_copy(fraction, out_frac, sems.at[1])
    store_green.start()
    store_frac.start()
    slopes = exact_dot(take_table[...], final[...], ((1,), (1,)))
    slopes = exact_dot(slopes, table_z[...]).reshape(predicted.shape)
    vel[0] = predicted[0] - slopes[0]
    vel[1] = predicted[1] - slopes[1]
    vel[2] = predicted[2] - 0.5 * (shift(slopes[2], 1, 2) - shift(slopes[2], -1, 2))
    store_vel = pltpu.make_async_copy(vel, out_vel, sems.at[2])
    store_vel.start()
    store_vel.wait()
    store_green.wait()
    store_frac.wait()


def fused_local(count_x, count_y, velocity, cauchy_green, labels):
    cells_x, cells_y, length_z = labels.shape
    devices = count_x * count_y
    rows = length_z // devices
    length_y = count_y * cells_y
    tables = spectral_tables(count_x, count_y, cells_x, cells_y, length_z)
    wide = (cells_x + 4) * length_y
    back = back_lanes(cells_x, cells_y)
    plane = (cells_y, length_z)
    real = functools.partial(pltpu.VMEM, dtype=jnp.float32)
    outputs = (
        jax.ShapeDtypeStruct(velocity.shape, jnp.float32),
        jax.ShapeDtypeStruct(cauchy_green.shape, jnp.float32),
        jax.ShapeDtypeStruct(labels.shape, jnp.float32),
    )
    handed = outputs + (
        jax.ShapeDtypeStruct((length_z, back), jnp.float32),
        jax.ShapeDtypeStruct(tables[0].shape, jnp.float32),
        jax.ShapeDtypeStruct(tables[6].shape, jnp.float32),
    )
    near = pl.BlockSpec(memory_space=pltpu.VMEM)
    far = pl.BlockSpec(memory_space=pltpu.HBM)
    scratch = [
        real(velocity.shape),
        real(cauchy_green.shape),
        pltpu.VMEM(labels.shape, jnp.int32),
        real(tables[1].shape[1:]),
        real(tables[2].shape),
        real(tables[3].shape),
        real(tables[4].shape),
        real(tables[5].shape[1:]),
        real(tables[7].shape),
        real((7, cells_x) + plane),
        real((7, cells_x) + plane),
        real((7, cells_x, 8, length_z)),
        real((3, 2 * cells_x, length_z)),
        real((6, 3) + plane),
        real((6, 3) + plane),
        pltpu.VMEM((3,) + plane, jnp.int32),
        pltpu.VMEM((3,) + plane, jnp.int32),
        real((3, 1) + plane),
        real((3, 1) + plane),
        real((7, cells_x, 8, length_z)),
        real((3, 2 * cells_x, length_z)),
        real((3, cells_x, 8, length_z)),
        real((6, cells_x) + plane),
        real((3, cells_x, 8, length_z)),
        real((3, 1) + plane),
        real((3, 1) + plane),
        real((3, cells_x, 8, length_z)),
        real((devices, rows, wide)),
        real((devices, rows, wide)),
        real((count_x * rows, wide)),
        real((devices, rows, back)),
        real((devices, rows, back)),
        pltpu.SemaphoreType.DMA((11,)),
        pltpu.SemaphoreType.DMA((2, 8)),
        pltpu.SemaphoreType.DMA((2, 3)),
        pltpu.SemaphoreType.DMA((devices,)),
        pltpu.SemaphoreType.DMA((devices,)),
        pltpu.SemaphoreType.DMA((devices,)),
        pltpu.SemaphoreType.DMA((devices,)),
        pltpu.SemaphoreType.DMA((2,)),
    ]
    made = pl.pallas_call(
        functools.partial(step_kernel, count_x, count_y),
        out_shape=handed,
        in_specs=[far] * 11,
        out_specs=(near,) * 6,
        scratch_shapes=scratch,
        compiler_params=pltpu.CompilerParams(
            collective_id=0, has_side_effects=True, vmem_limit_bytes=32 * 1024 * 1024
        ),
        name="membrane_step",
    )(*[
        pltpu.with_memory_space_constraint(value, pltpu.HBM)
        for value in (velocity, cauchy_green, labels, *map(jnp.asarray, tables))
    ])
    return tuple(
        pl.pallas_call(
            finish_kernel,
            out_shape=outputs,
            in_specs=[near] * 6,
            out_specs=(far,) * 3,
            scratch_shapes=[real(velocity.shape), pltpu.SemaphoreType.DMA((3,))],
            compiler_params=pltpu.CompilerParams(vmem_limit_bytes=16 * 1024 * 1024),
            name="finish_step",
        )(*made)
    )


def fits_fused(count_x, count_y, shape):
    _, length_x, length_y, length_z = shape
    cells_x, cells_y = length_x // count_x, length_y // count_y
    devices = count_x * count_y
    return (
        count_y == 2
        and count_x > 2
        and count_x & (count_x - 1) == 0
        and length_z % 128 == 0
        and length_z % devices == 0
        and length_z // devices in (4, 8)
        and cells_x >= 4
        and cells_y % 8 == 0
        and cells_y >= 8
        and (cells_x + 4) * length_y % 128 == 0
        and length_x * length_y <= 4096
    )


def solution(mesh):
    placed = (P(None, "gx", "gy", None), P(None, "gx", "gy", None), P("gx", "gy", None))
    count_x, count_y = mesh.shape["gx"], mesh.shape["gy"]

    def step(velocity, cauchy_green, labels):
        if fits_fused(count_x, count_y, velocity.shape):
            body = functools.partial(fused_local, count_x, count_y)
        else:
            body = local
        return jax.shard_map(
            body, mesh=mesh, in_specs=placed, out_specs=placed, check_vma=False
        )(velocity, cauchy_green, labels)

    return step
```

profile of v0, /device:TPU:0, one launch (start us, length us, event | category | flops | bytes accessed | tf_op | source)
XLA Modules:
  0.0 30.1 jit_solution(15591869047366556309)
XLA Ops:
  0.6 28.2 %membrane_step.1 = (f32[3,4,16,128]{3,2,1,0:T(8,128)S(1)}, f32[6,4,16,128]{3,2,1,0:T(8,128)S(1)}, f32[4,16,128]{2,1,0:T(8,128)S(1)}, f32[128,128]{1,0:T(8,128)S(...) custom-call(f32[3,4,16,128]{3,2,1,0:T(8,128)} %vel_far.1, f32[6,4,16,128]{3,2,1,0:T(8,128)} %green_far.1, ...), custom_call_target="tpu_custom_call" | custom-call | tf_op jit(solution)/shard_map/membrane_step/pallas_call | solution.py:917
  28.8 1.4 %finish_step.1 = (f32[3,4,16,128]{3,2,1,0:T(8,128)}, f32[6,4,16,128]{3,2,1,0:T(8,128)}, f32[4,16,128]{2,1,0:T(8,128)}) custom-call(f32[3,4,16,128]{3,2,1,0:T(8,128)S(1)} %get-tuple-element.9.predicted, f32[6,4,16,128]{3,2,1,0:T(8,128)S(1)} %get-tuple-element.10.green, f32[4,16,128]{2,1,0:T(8,128)S(1)} %get-tuple-element.11.fraction, ...), custom_call_target="tpu_custom_call" | custom-call | tf_op jit(solution)/shard_map/finish_step/pallas_call | solution.py:932
where the time goes:
time: 30.3 us; the launch traced here: 30.1 us
  Pallas kernels  29.5 us (97%)
  between operations  0.64 us (2%)
    pallas_call x1, Pallas kernels, fused_local(): pl.pallas_call(functools.partial(step_kernel, count_x, count_y), out_shap...  28.2 us
    pallas_call x1, Pallas kernels, fused_local(): pl.pallas_call(finish_kernel, out_shape=outputs, in_specs=[near] * 6, out...  1.35 us

commit v1 on v0

--- a/solution.py
+++ b/solution.py
@@ -327,6 +327,12 @@
     index = np.arange(length)
     sine = np.where(index % (length // 2) == 0, 0.0, np.sin(2.0 * np.pi / length * index))
     return sine * sine
+
+
+def split_table(table):
+    high = np.asarray(table, jnp.bfloat16)
+    low = np.asarray(table - np.asarray(high, np.float64), jnp.bfloat16)
+    return np.stack([high, low])
 
 
 def back_lanes(cells_x, cells_y):
@@ -383,17 +389,18 @@
     square_xy = np.repeat(sine_squares(length_x), rows)[:, None] + sine_squares(length_y)[None, :]
     square_z = sine_squares(length_z).reshape(devices, rows)
     square_z = np.tile(square_z, (1, 8 // rows))[:, :, None] * np.ones((1, 1, length_y))
-    made = (
-        table_z,
-        send_table.reshape(count_y, 6 * cells_x * cells_y, wide * length_y),
-        solve_in,
-        solve_out,
-        square_xy.reshape(-1, 8, length_y),
-        square_z,
-        take_table.reshape(3 * cells_x * cells_y, -1),
-        turn_table.reshape(length_y, count_y * near_y),
-    )
-    return tuple(np.asarray(table, np.float32) for table in made)
+    send_table = send_table.reshape(count_y, 6 * cells_x * cells_y, wide * length_y)
+    take_table = take_table.reshape(3 * cells_x * cells_y, -1)
+    return (
+        split_table(table_z),
+        np.moveaxis(split_table(send_table), 0, 1),
+        split_table(solve_in),
+        split_table(solve_out),
+        np.asarray(square_xy.reshape(-1, 8, length_y), np.float32),
+        np.asarray(square_z, np.float32),
+        np.asarray(take_table, jnp.bfloat16),
+        split_table(turn_table.reshape(length_y, count_y * near_y)),
+    )
 
 
 def shift(values, offset, axis):
@@ -447,14 +454,21 @@
     return values * (speed - shift(speed, -1, axis)) - (flux - shift(flux, -1, axis))
 
 
-def exact_dot(left, right, dims=((1,), (0,))):
+def split_values(values):
+    high = values.astype(jnp.bfloat16)
+    return high, (values - high.astype(jnp.float32)).astype(jnp.bfloat16)
+
+
+def narrow_dot(left, right, dims=((1,), (0,))):
     return lax.dot_general(
-        left,
-        right,
-        (dims, ((), ())),
-        precision=lax.Precision.HIGHEST,
-        preferred_element_type=jnp.float32,
-    )
+        left, right, (dims, ((), ())), preferred_element_type=jnp.float32
+    )
+
+
+def split_dot(left, right, dims=((1,), (0,))):
+    joined_left = jnp.concatenate([left[0], left[0], left[1]], axis=dims[0][0])
+    joined_right = jnp.concatenate([right[0], right[1], right[0]], axis=dims[1][0])
+    return narrow_dot(joined_left, joined_right, dims)
 
 
 def step_kernel(
@@ -512,11 +526,8 @@
     load_sem,
     halo_sem,
     stress_sem,
-    go_send,
-    go_recv,
-    back_send,
-    back_recv,
-    own_sem,
+    go_sem,
+    back_sem,
 ):
     cells_x, cells_y, length_z = labels.shape
     devices = count_x * count_y
@@ -732,15 +743,14 @@
     )
     for copy in loads[3:]:
         copy.wait()
-    modes_z = exact_dot(table_z[...], stacked, ((1,), (1,)))
-    modes_zy = exact_dot(modes_z, send_table[...])
+    modes_z = split_dot(table_z, split_values(stacked), ((1,), (1,)))
+    modes_zy = split_dot(split_values(modes_z), send_table)
     for n in range(devices):
         outbox[n] = modes_zy[n * rows : (n + 1) * rows]
 
     for target, device in others:
-        remote(outbox.at[target], inbox.at[me], go_send.at[target], go_recv.at[me], device).start()
-    keep = pltpu.make_async_copy(outbox.at[me], inbox.at[me], own_sem.at[0])
-    keep.start()
+        remote(outbox.at[target], inbox.at[me], go_sem.at[0], go_sem.at[1], device).start()
+    inbox[me] = outbox[me]
     stress_list = (
         (stress_pack, stress_side, over),
         (stress.at[:3, cells_x - 1 :], stress_low, right),
@@ -759,11 +769,8 @@
     green_function = jnp.where(live, (-1.0 / total) / jnp.where(live, norm, 1.0), 0.0)
     green_function = green_function.reshape(-1, length_y)
 
-    for source, device in reversed(others):
-        remote(
-            outbox.at[source], inbox.at[source], go_send.at[source], go_recv.at[source], device
-        ).wait()
-    keep.wait()
+    most = pl.ds(0, devices - 1)
+    remote(outbox.at[most], inbox.at[most], go_sem.at[0], go_sem.at[1], right).wait()
 
     for n in range(count_x):
         held = inbox[n * count_y]
@@ -773,8 +780,13 @@
     arranged = jnp.concatenate(
         [lines[:, n * length_y : (n + 1) * length_y] for n in range(wide)], axis=0
     )
-    pressure_modes = exact_dot(solve_in[...], arranged) * green_function
-    pressure = exact_dot(solve_out[...], exact_dot(pressure_modes, turn_table[...]))
+    pressure_modes = split_values(split_dot(solve_in, split_values(arranged)) * green_function)
+    turned = (
+        narrow_dot(pressure_modes[0], turn_table[0])
+        + narrow_dot(pressure_modes[0], turn_table[1])
+        + narrow_dot(pressure_modes[1], turn_table[0])
+    )
+    pressure = split_dot(solve_out, split_values(turned))
     height = count_x * rows
     near_y = cells_y + 2
     for m in range(count_y):
@@ -791,10 +803,9 @@
 
     for target, device in others:
         remote(
-            backbox.at[target], homebox.at[me], back_send.at[target], back_recv.at[me], device
+            backbox.at[target], homebox.at[me], back_sem.at[0], back_sem.at[1], device
         ).start()
-    stay = pltpu.make_async_copy(backbox.at[me], homebox.at[me], own_sem.at[1])
-    stay.start()
+    homebox[me] = backbox[me]
 
     for copy in edges:
         copy.wait()
@@ -812,11 +823,7 @@
         )
         out_vel[c] = vel[c] + time_step * pushed
 
-    for source, device in reversed(others):
-        remote(
-            backbox.at[source], homebox.at[source], back_send.at[source], back_recv.at[source], device
-        ).wait()
-    stay.wait()
+    remote(backbox.at[most], homebox.at[most], back_sem.at[0], back_sem.at[1], right).wait()
     for n in range(devices):
         final[n * rows : (n + 1) * rows] = homebox[n]
 
@@ -838,8 +845,9 @@
     store_frac = pltpu.make_async_copy(fraction, out_frac, sems.at[1])
     store_green.start()
     store_frac.start()
-    slopes = exact_dot(take_table[...], final[...], ((1,), (1,)))
-    slopes = exact_dot(slopes, table_z[...]).reshape(predicted.shape)
+    taken = jnp.concatenate([take_table[...], take_table[...]], axis=1)
+    slopes = narrow_dot(taken, jnp.concatenate(split_values(final[...]), axis=1), ((1,), (1,)))
+    slopes = split_dot(split_values(slopes), table_z).reshape(predicted.shape)
     vel[0] = predicted[0] - slopes[0]
     vel[1] = predicted[1] - slopes[1]
     vel[2] = predicted[2] - 0.5 * (shift(slopes[2], 1, 2) - shift(slopes[2], -1, 2))
@@ -867,8 +875,8 @@
     )
     handed = outputs + (
         jax.ShapeDtypeStruct((length_z, back), jnp.float32),
-        jax.ShapeDtypeStruct(tables[0].shape, jnp.float32),
-        jax.ShapeDtypeStruct(tables[6].shape, jnp.float32),
+        jax.ShapeDtypeStruct(tables[0].shape, jnp.bfloat16),
+        jax.ShapeDtypeStruct(tables[6].shape, jnp.bfloat16),
     )
     near = pl.BlockSpec(memory_space=pltpu.VMEM)
     far = pl.BlockSpec(memory_space=pltpu.HBM)
@@ -876,12 +884,12 @@
         real(velocity.shape),
         real(cauchy_green.shape),
         pltpu.VMEM(labels.shape, jnp.int32),
-        real(tables[1].shape[1:]),
-        real(tables[2].shape),
-        real(tables[3].shape),
+        pltpu.VMEM(tables[1].shape[1:], jnp.bfloat16),
+        pltpu.VMEM(tables[2].shape, jnp.bfloat16),
+        pltpu.VMEM(tables[3].shape, jnp.bfloat16),
         real(tables[4].shape),
         real(tables[5].shape[1:]),
-        real(tables[7].shape),
+        pltpu.VMEM(tables[7].shape, jnp.bfloat16),
         real((7, cells_x) + plane),
         real((7, cells_x) + plane),
         real((7, cells_x, 8, length_z)),
@@ -908,10 +916,7 @@
         pltpu.SemaphoreType.DMA((11,)),
         pltpu.SemaphoreType.DMA((2, 8)),
         pltpu.SemaphoreType.DMA((2, 3)),
-        pltpu.SemaphoreType.DMA((devices,)),
-        pltpu.SemaphoreType.DMA((devices,)),
-        pltpu.SemaphoreType.DMA((devices,)),
-        pltpu.SemaphoreType.DMA((devices,)),
+        pltpu.SemaphoreType.DMA((2,)),
         pltpu.SemaphoreType.DMA((2,)),
     ]
     made = pl.pallas_call(

time: 30.3 us -> 27.7 us (0.914)
  Pallas kernels: 29.5 us -> 26.9 us
    pallas_call x1, Pallas kernels: 28.2 us -> 25.8 us  [fused_local(): pl.pallas_call(functools.partial(step_kernel, count_x, count_y), out_shap...]
where the time goes in v1:
time: 27.7 us; the launch traced here: 27.5 us
  Pallas kernels  26.9 us (97%)
  between operations  0.64 us (2%)
    pallas_call x1, Pallas kernels, fused_local(): pl.pallas_call(functools.partial(step_kernel, count_x, count_y), out_shap...  25.8 us
    pallas_call x1, Pallas kernels, fused_local(): pl.pallas_call(finish_kernel, out_shape=outputs, in_specs=[near] * 6, out...  1.1 us

profile of v1, /device:TPU:0, one launch (start us, length us, event | category | flops | bytes accessed | tf_op | source)
XLA Modules:
  0.0 27.5 jit_solution(4827228656993182721)
XLA Ops:
  0.6 25.8 %membrane_step.1 = (f32[3,4,16,128]{3,2,1,0:T(8,128)S(1)}, f32[6,4,16,128]{3,2,1,0:T(8,128)S(1)}, f32[4,16,128]{2,1,0:T(8,128)S(1)}, f32[128,128]{1,0:T(8,128)S(...) custom-call(f32[3,4,16,128]{3,2,1,0:T(8,128)} %vel_far.1, f32[6,4,16,128]{3,2,1,0:T(8,128)} %green_far.1, ...), custom_call_target="tpu_custom_call" | custom-call | tf_op jit(solution)/shard_map/membrane_step/pallas_call | solution.py:922
  26.4 1.1 %finish_step.1 = (f32[3,4,16,128]{3,2,1,0:T(8,128)}, f32[6,4,16,128]{3,2,1,0:T(8,128)}, f32[4,16,128]{2,1,0:T(8,128)}) custom-call(f32[3,4,16,128]{3,2,1,0:T(8,128)S(1)} %get-tuple-element.9.predicted, f32[6,4,16,128]{3,2,1,0:T(8,128)S(1)} %get-tuple-element.10.green, f32[4,16,128]{2,1,0:T(8,128)S(1)} %get-tuple-element.11.fraction, ...), custom_call_target="tpu_custom_call" | custom-call | tf_op jit(solution)/shard_map/finish_step/pallas_call | solution.py:937

commit v2 on v1

--- a/solution.py
+++ b/solution.py
@@ -15,6 +15,7 @@
 weno_eps = 1e-06
 pair_list = ((0, 0), (1, 1), (2, 2), (0, 1), (0, 2), (1, 2))
 slot_table = ((0, 3, 4), (3, 1, 5), (4, 5, 2))
+plane_bits = 2
 
 
 def padded_2(block, sides, width):
@@ -528,6 +529,8 @@
     stress_sem,
     go_sem,
     back_sem,
+    rung_sem,
+    edge_flux,
 ):
     cells_x, cells_y, length_z = labels.shape
     devices = count_x * count_y
@@ -553,8 +556,21 @@
             peer_y = 1 - me_y
         others.append((peer_x * count_y + peer_y, (peer_x, peer_y)))
 
+    def toggled(mask, flip):
+        place = me_x
+        for bit, turn in enumerate(turns):
+            if mask >> bit & 1:
+                place = place + turn
+        return (place, 1 - me_y if flip else me_y)
+
+    right = (lax.rem(me_x + 1, count_x), me_y)
+    left = (lax.rem(me_x + count_x - 1, count_x), me_y)
+    over = (me_x, 1 - me_y)
+    rungs = [toggled(1 << bit, False) for bit in range(plane_bits, len(turns))]
+    mates = [toggled(mask, flip) for mask in range(1 << plane_bits) for flip in (0, 1)][1:]
+    greeted = [left, right] + rungs + mates
     barrier = pltpu.get_barrier_semaphore()
-    for _, device in others:
+    for device in greeted:
         pl.semaphore_signal(barrier, inc=1, device_id=device, device_id_type=mesh_type)
 
     load_list = (
@@ -596,11 +612,17 @@
             vel_pack[c, 2 * x + 1] = vel[c, x, cells_y - 1]
             vel_side[c, x] = jnp.zeros((8, length_z), jnp.float32)
 
-    pl.semaphore_wait(barrier, devices - 1)
-
-    right = (lax.rem(me_x + 1, count_x), me_y)
-    left = (lax.rem(me_x + count_x - 1, count_x), me_y)
-    over = (me_x, lax.rem(me_y + 1, count_y))
+    def sweep_z(c, carry):
+        for x in range(cells_x):
+            moved[c, x] = ring_sweep(field[c, x], vel[2, x], 1)
+        return carry
+
+    @pl.when(me_x == 0)
+    def _():
+        lax.fori_loop(0, 7, sweep_z, 0)
+
+    pl.semaphore_wait(barrier, len(greeted))
+
 
     def remote(source, target, send_sem, recv_sem, device):
         return pltpu.make_async_remote_copy(
@@ -615,12 +637,15 @@
     halo_list = (
         (vel_pack, vel_near, over),
         (pack, side, over),
+        (vel.at[:, :1], high_vel, left),
+        (labels.at[:3], high_label, left),
+        *[
+            (green.at[n : n + 2, :3], high_green.at[n : n + 2], left)
+            for n in range(0, 6, 2)
+        ],
+        (vel.at[:, cells_x - 1 :], low_vel, right),
+        (labels.at[cells_x - 3 :], low_label, right),
         (green.at[:, cells_x - 3 :], low_green, right),
-        (green.at[:, :3], high_green, left),
-        (vel.at[:, cells_x - 1 :], low_vel, right),
-        (vel.at[:, :1], high_vel, left),
-        (labels.at[cells_x - 3 :], low_label, right),
-        (labels.at[:3], high_label, left),
     )
     halos = [
         remote(source, target, halo_sem.at[0, n], halo_sem.at[1, n], device)
@@ -629,18 +654,24 @@
     for copy in halos:
         copy.start()
 
-    def sweep_z(c, carry):
-        for x in range(cells_x):
-            moved[c, x] = ring_sweep(field[c, x], vel[2, x], 1)
-        return carry
-
-    lax.fori_loop(0, 7, sweep_z, 0)
+    def tell(n):
+        pl.semaphore_signal(rung_sem.at[n], inc=1, device_id=rungs[n], device_id_type=mesh_type)
+
+    if rungs:
+        tell(0)
+
+    @pl.when(me_x != 0)
+    def _():
+        lax.fori_loop(0, 7, sweep_z, 0)
 
     halos[0].wait()
     for c in range(3):
         for x in range(cells_x):
             vel_side[c, x, 0] = vel_near[c, 2 * x]
             vel_side[c, x, 7] = vel_near[c, 2 * x + 1]
+    for n in range(1, len(rungs)):
+        pl.semaphore_wait(rung_sem.at[n - 1], 1)
+        tell(n)
     halos[1].wait()
 
     def sweep_y(c, carry):
@@ -652,39 +683,72 @@
 
     lax.fori_loop(0, 7, sweep_y, 0)
 
-    for copy in halos[2:]:
+    for copy in halos[7:]:
         copy.wait()
 
     def wide_vel(c):
         return jnp.concatenate([low_vel[c], vel[c], high_vel[c]], axis=0)
 
-    def sweep_x(values, c):
-        advecting = [low_vel[0, 0]] + [vel[0, x] for x in range(cells_x)] + [high_vel[0, 0]]
-        flux = []
-        speeds = []
-        for face in range(cells_x + 1):
-            speed = 0.5 * (advecting[face] + advecting[face + 1])
-            speeds.append(speed)
-            flux.append(upwind_flux(lambda o: values[face + 2 + o], speed))
-        for x in range(cells_x):
-            moved[c, x] = (
-                moved[c, x]
-                + values[x + 3] * (speeds[x + 1] - speeds[x])
-                - (flux[x + 1] - flux[x])
-            )
-
-    def sweep_green(c, carry):
-        values = [low_green[c, n] for n in range(3)]
-        values += [field[c, x] for x in range(cells_x)]
-        values += [high_green[c, n] for n in range(3)]
-        sweep_x(values, c)
+    def plane_at(c, n):
+        if n < 3:
+            return low_label[n].astype(jnp.float32) * 0.25 if c is None else low_green[c, n]
+        if n < cells_x + 3:
+            return field[6 if c is None else c, n - 3]
+        n = n - cells_x - 3
+        return high_label[n].astype(jnp.float32) * 0.25 if c is None else high_green[c, n]
+
+    def face_speed(face):
+        before = low_vel[0, 0] if face == 0 else vel[0, face - 1]
+        after = high_vel[0, 0] if face == cells_x else vel[0, face]
+        return 0.5 * (before + after)
+
+    split_face = cells_x - 2
+
+    def face_flux_x(c, face, speed):
+        return upwind_flux(lambda o: plane_at(c, face + 2 + o), speed)
+
+    def sweep_faces(c, first, last, speed_low, flux_low):
+        slot = 6 if c is None else c
+        for face in range(first, last):
+            speed = face_speed(face)
+            flux = face_flux_x(c, face, speed)
+            if flux_low is not None:
+                moved[slot, face - 1] = (
+                    moved[slot, face - 1]
+                    + plane_at(c, face + 2) * (speed - speed_low)
+                    - (flux - flux_low)
+                )
+            speed_low, flux_low = speed, flux
+        return flux_low
+
+    def sweep_low(c):
+        edge_flux[6 if c is None else c] = sweep_faces(c, 0, split_face, None, None)
+
+    def sweep_high(c):
+        sweep_faces(
+            c,
+            split_face,
+            cells_x + 1,
+            face_speed(split_face - 1),
+            edge_flux[6 if c is None else c],
+        )
+
+    def low_step(c, carry):
+        sweep_low(c)
         return carry
 
-    lax.fori_loop(0, 6, sweep_green, 0)
-    values = [low_label[n].astype(jnp.float32) * 0.25 for n in range(3)]
-    values += [field[6, x] for x in range(cells_x)]
-    values += [high_label[n].astype(jnp.float32) * 0.25 for n in range(3)]
-    sweep_x(values, 6)
+    def high_step(c, carry):
+        sweep_high(c)
+        return carry
+
+    lax.fori_loop(0, 6, low_step, 0)
+    sweep_low(None)
+    halos[2].wait()
+    halos[3].wait()
+    sweep_high(None)
+    for n in range(3):
+        halos[4 + n].wait()
+        lax.fori_loop(2 * n, 2 * n + 2, high_step, 0)
 
     def central_z(block):
         return 0.5 * (shift(block, 1, 2) - shift(block, -1, 2))
@@ -748,6 +812,8 @@
     for n in range(devices):
         outbox[n] = modes_zy[n * rows : (n + 1) * rows]
 
+    if rungs:
+        pl.semaphore_wait(rung_sem.at[len(rungs) - 1], 1)
     for target, device in others:
         remote(outbox.at[target], inbox.at[me], go_sem.at[0], go_sem.at[1], device).start()
     inbox[me] = outbox[me]
@@ -914,10 +980,12 @@
         real((devices, rows, back)),
         real((devices, rows, back)),
         pltpu.SemaphoreType.DMA((11,)),
-        pltpu.SemaphoreType.DMA((2, 8)),
+        pltpu.SemaphoreType.DMA((2, 10)),
         pltpu.SemaphoreType.DMA((2, 3)),
         pltpu.SemaphoreType.DMA((2,)),
         pltpu.SemaphoreType.DMA((2,)),
+        pltpu.SemaphoreType.REGULAR((max(count_x.bit_length() - 1 - plane_bits, 1),)),
+        real((7,) + plane),
     ]
     made = pl.pallas_call(
         functools.partial(step_kernel, count_x, count_y),

time: 27.7 us -> 25.6 us (0.924)
  Pallas kernels: 26.9 us -> 24.8 us
    pallas_call x1, Pallas kernels: 25.8 us -> 23.7 us  [fused_local(): pl.pallas_call(functools.partial(step_kernel, count_x, count_y), out_shap...]
where the time goes in v2:
time: 25.6 us; the launch traced here: 25.4 us
  Pallas kernels  24.8 us (97%)
  between operations  0.64 us (2%)
    pallas_call x1, Pallas kernels, fused_local(): pl.pallas_call(functools.partial(step_kernel, count_x, count_y), out_shap...  23.7 us
    pallas_call x1, Pallas kernels, fused_local(): pl.pallas_call(finish_kernel, out_shape=outputs, in_specs=[near] * 6, out...  1.1 us

profile of v2, /device:TPU:0, one launch (start us, length us, event | category | flops | bytes accessed | tf_op | source)
XLA Modules:
  0.0 25.4 jit_solution(1566174071367728666)
XLA Ops:
  0.6 23.7 %membrane_step.1 = (f32[3,4,16,128]{3,2,1,0:T(8,128)S(1)}, f32[6,4,16,128]{3,2,1,0:T(8,128)S(1)}, f32[4,16,128]{2,1,0:T(8,128)S(1)}, f32[128,128]{1,0:T(8,128)S(...) custom-call(f32[3,4,16,128]{3,2,1,0:T(8,128)} %vel_far.1, f32[6,4,16,128]{3,2,1,0:T(8,128)} %green_far.1, ...), custom_call_target="tpu_custom_call" | custom-call | tf_op jit(solution)/shard_map/membrane_step/pallas_call | solution.py:990
  24.3 1.1 %finish_step.1 = (f32[3,4,16,128]{3,2,1,0:T(8,128)}, f32[6,4,16,128]{3,2,1,0:T(8,128)}, f32[4,16,128]{2,1,0:T(8,128)}) custom-call(f32[3,4,16,128]{3,2,1,0:T(8,128)S(1)} %get-tuple-element.9.predicted, f32[6,4,16,128]{3,2,1,0:T(8,128)S(1)} %get-tuple-element.10.green, f32[4,16,128]{2,1,0:T(8,128)S(1)} %get-tuple-element.11.fraction, ...), custom_call_target="tpu_custom_call" | custom-call | tf_op jit(solution)/shard_map/finish_step/pallas_call | solution.py:1005

commit v3 on v2

--- a/solution.py
+++ b/solution.py
@@ -352,20 +352,33 @@
         {-2: 0.25, 0: -0.5, 2: 0.25},
     )
     field_orders = ((2, 0), (1, 1), (1, 0), (0, 2), (0, 1), (0, 0))
-    send_table = np.zeros((count_y, 6, cells_x, cells_y, wide, length_y))
+    lanes = wide * cells_y
+    send_table = np.zeros((6, cells_x, cells_y, lanes + 128))
+    outside = {}
+    for field, (order_x, order_y) in enumerate(field_orders):
+        for x, y in np.ndindex(cells_x, cells_y):
+            for offset_x, weight_x in stencils[order_x].items():
+                for offset_y, weight_y in stencils[order_y].items():
+                    column, line = x + 2 + offset_x, y + offset_y
+                    target = send_table[field, x, y]
+                    if 0 <= line < cells_y:
+                        target[column * cells_y + line] += weight_x * weight_y
+                    else:
+                        spot = outside.setdefault((column, line), len(outside))
+                        target[lanes + spot :: 128 // rows] += weight_x * weight_y
+    spread_table = np.zeros((count_y, 2, lanes, wide, length_y))
+    for block in range(count_y):
+        for column, line in np.ndindex(wide, cells_y):
+            place = block * cells_y + line
+            spread_table[block, 0, column * cells_y + line, column] = table_y[place]
+        for (column, line), spot in outside.items():
+            place = (block * cells_y + line) % length_y
+            spread_table[block, 1, spot :: 128 // rows, column] = table_y[place]
+    spread_table = np.moveaxis(spread_table, 0, 1)
     near_x, near_y = cells_x + 2, cells_y + 2
     take_table = np.zeros((3, cells_x, cells_y, back_lanes(cells_x, cells_y)))
     turn_table = np.zeros((length_y, count_y, near_y))
     for block in range(count_y):
-        place = block * cells_y + np.arange(cells_y)
-        along = [
-            sum(w * table_y[(place + o) % length_y] for o, w in stencil.items())
-            for stencil in stencils
-        ]
-        for field, (order_x, order_y) in enumerate(field_orders):
-            for cell in range(cells_x):
-                for offset, weight in stencils[order_x].items():
-                    send_table[block, field, cell, :, cell + 2 + offset] += weight * along[order_y]
         ring = (block * cells_y + np.arange(near_y) - 1) % length_y
         turn_table[:, block] = table_y[:, ring]
     for x in range(cells_x):
@@ -390,17 +403,19 @@
     square_xy = np.repeat(sine_squares(length_x), rows)[:, None] + sine_squares(length_y)[None, :]
     square_z = sine_squares(length_z).reshape(devices, rows)
     square_z = np.tile(square_z, (1, 8 // rows))[:, :, None] * np.ones((1, 1, length_y))
-    send_table = send_table.reshape(count_y, 6 * cells_x * cells_y, wide * length_y)
+    send_table = send_table.reshape(6 * cells_x * cells_y, lanes + 128)
+    spread_table = spread_table.reshape(-1, wide * length_y)
     take_table = take_table.reshape(3 * cells_x * cells_y, -1)
     return (
         split_table(table_z),
-        np.moveaxis(split_table(send_table), 0, 1),
+        np.asarray(send_table, jnp.bfloat16),
         split_table(solve_in),
         split_table(solve_out),
         np.asarray(square_xy.reshape(-1, 8, length_y), np.float32),
         np.asarray(square_z, np.float32),
         np.asarray(take_table, jnp.bfloat16),
         split_table(turn_table.reshape(length_y, count_y * near_y)),
+        split_table(spread_table),
     )
 
 
@@ -486,6 +501,7 @@
     square_z_far,
     take_table_far,
     turn_table_far,
+    spread_table_far,
     out_vel,
     out_green,
     out_frac,
@@ -501,12 +517,13 @@
     square_xy,
     square_z,
     turn_table,
+    spread_table,
     field,
     moved,
     pack,
     vel_pack,
-    low_green,
-    high_green,
+    low_wide,
+    high_wide,
     low_label,
     high_label,
     low_vel,
@@ -521,7 +538,6 @@
     stress_side,
     outbox,
     inbox,
-    lines,
     backbox,
     homebox,
     load_sem,
@@ -537,6 +553,7 @@
     rows = length_z // devices
     length_y = count_y * cells_y
     wide = cells_x + 4
+    lanes = wide * cells_y
     me_x = lax.axis_index("gx")
     me_y = lax.axis_index("gy")
     me = me_x * count_y + me_y
@@ -578,13 +595,14 @@
         (green_far, green),
         (labels_far, labels),
         (table_z_far, table_z),
-        (send_table_far.at[me_y], send_table),
+        (send_table_far, send_table),
         (square_xy_far, square_xy),
         (square_z_far.at[me], square_z),
         (solve_in_far, solve_in),
         (solve_out_far, solve_out),
         (take_table_far, take_table),
         (turn_table_far, turn_table),
+        (spread_table_far, spread_table),
     )
     loads = [
         pltpu.make_async_copy(source, target, load_sem.at[n])
@@ -634,18 +652,26 @@
             device_id_type=mesh_type,
         )
 
+    y_pieces = ((0, 3), (3, 5), (5, 7))
+    x_pieces = ((0, 2), (2, 4), (4, 6))
     halo_list = (
         (vel_pack, vel_near, over),
-        (pack, side, over),
+        *[
+            (pack.at[first:last], side.at[first:last], over)
+            for first, last in y_pieces
+        ],
         (vel.at[:, :1], high_vel, left),
         (labels.at[:3], high_label, left),
         *[
-            (green.at[n : n + 2, :3], high_green.at[n : n + 2], left)
-            for n in range(0, 6, 2)
+            (green.at[first:last, :3], high_wide.at[first:last], left)
+            for first, last in x_pieces
         ],
         (vel.at[:, cells_x - 1 :], low_vel, right),
         (labels.at[cells_x - 3 :], low_label, right),
-        (green.at[:, cells_x - 3 :], low_green, right),
+        *[
+            (green.at[first:last, cells_x - 3 :], low_wide.at[first:last], right)
+            for first, last in x_pieces
+        ],
     )
     halos = [
         remote(source, target, halo_sem.at[0, n], halo_sem.at[1, n], device)
@@ -653,6 +679,7 @@
     ]
     for copy in halos:
         copy.start()
+    y_halos, high_halos, low_halos = halos[1:4], halos[4:9], halos[9:14]
 
     def tell(n):
         pl.semaphore_signal(rung_sem.at[n], inc=1, device_id=rungs[n], device_id_type=mesh_type)
@@ -672,8 +699,6 @@
     for n in range(1, len(rungs)):
         pl.semaphore_wait(rung_sem.at[n - 1], 1)
         tell(n)
-    halos[1].wait()
-
     def sweep_y(c, carry):
         for x in range(cells_x):
             values = jnp.concatenate([field[c, x], side[c, x]], axis=0)
@@ -681,74 +706,96 @@
             moved[c, x] = moved[c, x] + ring_sweep(values, advecting, 0)[:cells_y]
         return carry
 
-    lax.fori_loop(0, 7, sweep_y, 0)
-
-    for copy in halos[7:]:
+    for copy, (first, last) in zip(y_halos, y_pieces):
         copy.wait()
-
-    def wide_vel(c):
-        return jnp.concatenate([low_vel[c], vel[c], high_vel[c]], axis=0)
-
-    def plane_at(c, n):
-        if n < 3:
-            return low_label[n].astype(jnp.float32) * 0.25 if c is None else low_green[c, n]
-        if n < cells_x + 3:
-            return field[6 if c is None else c, n - 3]
-        n = n - cells_x - 3
-        return high_label[n].astype(jnp.float32) * 0.25 if c is None else high_green[c, n]
+        lax.fori_loop(first, last, sweep_y, 0)
 
     def face_speed(face):
         before = low_vel[0, 0] if face == 0 else vel[0, face - 1]
         after = high_vel[0, 0] if face == cells_x else vel[0, face]
         return 0.5 * (before + after)
 
-    split_face = cells_x - 2
-
-    def face_flux_x(c, face, speed):
-        return upwind_flux(lambda o: plane_at(c, face + 2 + o), speed)
-
-    def sweep_faces(c, first, last, speed_low, flux_low):
-        slot = 6 if c is None else c
+    def plane_at(c, n):
+        if n < 3:
+            return low_wide[c, n]
+        if n < cells_x + 3:
+            return field[c, n - 3]
+        return high_wide[c, n - cells_x - 3]
+
+    def settle(c, x, speeds, fluxes):
+        moved[c, x] = (
+            moved[c, x]
+            + plane_at(c, x + 3) * (speeds[1] - speeds[0])
+            - (fluxes[1] - fluxes[0])
+        )
+
+    def sweep_faces(c, first, last):
+        before = None
+        opening = None
         for face in range(first, last):
             speed = face_speed(face)
-            flux = face_flux_x(c, face, speed)
-            if flux_low is not None:
-                moved[slot, face - 1] = (
-                    moved[slot, face - 1]
-                    + plane_at(c, face + 2) * (speed - speed_low)
-                    - (flux - flux_low)
-                )
-            speed_low, flux_low = speed, flux
-        return flux_low
-
-    def sweep_low(c):
-        edge_flux[6 if c is None else c] = sweep_faces(c, 0, split_face, None, None)
-
-    def sweep_high(c):
-        sweep_faces(
-            c,
-            split_face,
-            cells_x + 1,
-            face_speed(split_face - 1),
-            edge_flux[6 if c is None else c],
-        )
-
-    def low_step(c, carry):
-        sweep_low(c)
+            flux = upwind_flux(lambda o: plane_at(c, face + 2 + o), speed)
+            if before is None:
+                opening = (speed, flux)
+            else:
+                settle(c, face - 1, (before[0], speed), (before[1], flux))
+            before = (speed, flux)
+        return opening, before
+
+    def low_first(c, carry):
+        edge_flux[c] = sweep_faces(c, 0, middle)[1][1]
         return carry
 
-    def high_step(c, carry):
-        sweep_high(c)
+    def high_last(c, carry):
+        opening, _ = sweep_faces(c, middle, cells_x + 1)
+        speed = face_speed(middle - 1)
+        settle(c, middle - 1, (speed, opening[0]), (edge_flux[c], opening[1]))
         return carry
 
-    lax.fori_loop(0, 6, low_step, 0)
-    sweep_low(None)
-    halos[2].wait()
-    halos[3].wait()
-    sweep_high(None)
-    for n in range(3):
-        halos[4 + n].wait()
-        lax.fori_loop(2 * n, 2 * n + 2, high_step, 0)
+    def high_first(c, carry):
+        edge_flux[c] = sweep_faces(c, middle + 1, cells_x + 1)[0][1]
+        return carry
+
+    def low_last(c, carry):
+        _, closing = sweep_faces(c, 0, middle + 1)
+        speed = face_speed(middle + 1)
+        settle(c, middle, (closing[0], speed), (closing[1], edge_flux[c]))
+        return carry
+
+    middle = cells_x - 2
+
+    def take_low(step):
+        low_halos[0].wait()
+        low_halos[1].wait()
+        low_wide[6] = low_label[...].astype(jnp.float32) * 0.25
+        lax.fori_loop(6, 7, step, 0)
+        for copy, (first, last) in zip(low_halos[2:], x_pieces):
+            copy.wait()
+            lax.fori_loop(first, last, step, 0)
+
+    def take_high(step):
+        high_halos[0].wait()
+        high_halos[1].wait()
+        high_wide[6] = high_label[...].astype(jnp.float32) * 0.25
+        lax.fori_loop(6, 7, step, 0)
+        for copy, (first, last) in zip(high_halos[2:], x_pieces):
+            copy.wait()
+            lax.fori_loop(first, last, step, 0)
+
+    odd = lax.rem(me_x, 2) == 1
+
+    @pl.when(odd)
+    def _():
+        take_low(low_first)
+        take_high(high_last)
+
+    @pl.when(jnp.logical_not(odd))
+    def _():
+        take_high(high_first)
+        take_low(low_last)
+
+    def wide_vel(c):
+        return jnp.concatenate([low_vel[c], vel[c], high_vel[c]], axis=0)
 
     def central_z(block):
         return 0.5 * (shift(block, 1, 2) - shift(block, -1, 2))
@@ -805,12 +852,24 @@
     stacked = jnp.concatenate(
         [part.reshape(cells_x * cells_y, length_z) for part in parts], axis=0
     )
+    def own_slot(values):
+        row_slot = lax.rem(lax.broadcasted_iota(jnp.int32, values.shape, 0), rows)
+        lane_slot = lax.broadcasted_iota(jnp.int32, values.shape, 1) // (128 // rows)
+        return jnp.where(row_slot == lane_slot, values, 0.0)
+
     for copy in loads[3:]:
         copy.wait()
     modes_z = split_dot(table_z, split_values(stacked), ((1,), (1,)))
-    modes_zy = split_dot(split_values(modes_z), send_table)
+    weights = send_table[...]
+    sent = narrow_dot(
+        jnp.concatenate(split_values(modes_z), axis=1), jnp.concatenate([weights, weights], axis=0)
+    )
+    fringe = own_slot(sent[:, lanes:])
+    fringe = fringe + shift(fringe, 1, 0)
+    fringe = fringe + shift(fringe, 2, 0)
     for n in range(devices):
-        outbox[n] = modes_zy[n * rows : (n + 1) * rows]
+        outbox[n, :rows] = sent[n * rows : (n + 1) * rows, :lanes]
+        outbox[n, rows] = fringe[n * rows]
 
     if rungs:
         pl.semaphore_wait(rung_sem.at[len(rungs) - 1], 1)
@@ -838,11 +897,16 @@
     most = pl.ds(0, devices - 1)
     remote(outbox.at[most], inbox.at[most], go_sem.at[0], go_sem.at[1], right).wait()
 
-    for n in range(count_x):
-        held = inbox[n * count_y]
-        for m in range(1, count_y):
-            held = held + inbox[n * count_y + m]
-        lines[n * rows : (n + 1) * rows] = held
+    blocks = [
+        jnp.concatenate([inbox[n * count_y + m, :rows] for n in range(count_x)], axis=0)
+        for m in range(count_y)
+    ]
+    for m in range(count_y):
+        fringe = [
+            jnp.broadcast_to(inbox[n * count_y + m, rows:], (rows, lanes)) for n in range(count_x)
+        ]
+        blocks.append(own_slot(jnp.concatenate(fringe, axis=0)))
+    lines = split_dot(split_values(jnp.concatenate(blocks, axis=1)), spread_table)
     arranged = jnp.concatenate(
         [lines[:, n * length_y : (n + 1) * length_y] for n in range(wide)], axis=0
     )
@@ -930,7 +994,7 @@
     rows = length_z // devices
     length_y = count_y * cells_y
     tables = spectral_tables(count_x, count_y, cells_x, cells_y, length_z)
-    wide = (cells_x + 4) * length_y
+    lanes = (cells_x + 4) * cells_y
     back = back_lanes(cells_x, cells_y)
     plane = (cells_y, length_z)
     real = functools.partial(pltpu.VMEM, dtype=jnp.float32)
@@ -950,18 +1014,19 @@
         real(velocity.shape),
         real(cauchy_green.shape),
         pltpu.VMEM(labels.shape, jnp.int32),
-        pltpu.VMEM(tables[1].shape[1:], jnp.bfloat16),
+        pltpu.VMEM(tables[1].shape, jnp.bfloat16),
         pltpu.VMEM(tables[2].shape, jnp.bfloat16),
         pltpu.VMEM(tables[3].shape, jnp.bfloat16),
         real(tables[4].shape),
         real(tables[5].shape[1:]),
         pltpu.VMEM(tables[7].shape, jnp.bfloat16),
+        pltpu.VMEM(tables[8].shape, jnp.bfloat16),
         real((7, cells_x) + plane),
         real((7, cells_x) + plane),
         real((7, cells_x, 8, length_z)),
         real((3, 2 * cells_x, length_z)),
-        real((6, 3) + plane),
-        real((6, 3) + plane),
+        real((7, 3) + plane),
+        real((7, 3) + plane),
         pltpu.VMEM((3,) + plane, jnp.int32),
         pltpu.VMEM((3,) + plane, jnp.int32),
         real((3, 1) + plane),
@@ -974,13 +1039,12 @@
         real((3, 1) + plane),
         real((3, 1) + plane),
         real((3, cells_x, 8, length_z)),
-        real((devices, rows, wide)),
-        real((devices, rows, wide)),
-        real((count_x * rows, wide)),
+        real((devices, rows + 1, lanes)),
+        real((devices, rows + 1, lanes)),
         real((devices, rows, back)),
         real((devices, rows, back)),
-        pltpu.SemaphoreType.DMA((11,)),
-        pltpu.SemaphoreType.DMA((2, 10)),
+        pltpu.SemaphoreType.DMA((12,)),
+        pltpu.SemaphoreType.DMA((2, 14)),
         pltpu.SemaphoreType.DMA((2, 3)),
         pltpu.SemaphoreType.DMA((2,)),
         pltpu.SemaphoreType.DMA((2,)),
@@ -990,7 +1054,7 @@
     made = pl.pallas_call(
         functools.partial(step_kernel, count_x, count_y),
         out_shape=handed,
-        in_specs=[far] * 11,
+        in_specs=[far] * 12,
         out_specs=(near,) * 6,
         scratch_shapes=scratch,
         compiler_params=pltpu.CompilerParams(
@@ -1024,7 +1088,9 @@
         and count_x & (count_x - 1) == 0
         and length_z % 128 == 0
         and length_z % devices == 0
-        and length_z // devices in (4, 8)
+        and length_z // devices == 4
+        and (cells_x + 4) * cells_y == 128
+        and cells_x <= 7
         and cells_x >= 4
         and cells_y % 8 == 0
         and cells_y >= 8

time: 25.6 us -> 24.8 us (0.969)
  Pallas kernels: 24.8 us -> 24 us
    pallas_call x1, Pallas kernels: 23.7 us -> 22.9 us  [fused_local(): pl.pallas_call(functools.partial(step_kernel, count_x, count_y), out_shap...]
where the time goes in v3:
time: 24.8 us; the launch traced here: 24.7 us
  Pallas kernels  24 us (97%)
  between operations  0.64 us (3%)
    pallas_call x1, Pallas kernels, fused_local(): pl.pallas_call(functools.partial(step_kernel, count_x, count_y), out_shap...  22.9 us
    pallas_call x1, Pallas kernels, fused_local(): pl.pallas_call(finish_kernel, out_shape=outputs, in_specs=[near] * 6, out...  1.1 us

profile of v3, /device:TPU:0, one launch (start us, length us, event | category | flops | bytes accessed | tf_op | source)
XLA Modules:
  0.0 24.7 jit_solution(16929826304380776356)
XLA Ops:
  0.6 22.9 %membrane_step.1 = (f32[3,4,16,128]{3,2,1,0:T(8,128)S(1)}, f32[6,4,16,128]{3,2,1,0:T(8,128)S(1)}, f32[4,16,128]{2,1,0:T(8,128)S(1)}, f32[128,128]{1,0:T(8,128)S(...) custom-call(f32[3,4,16,128]{3,2,1,0:T(8,128)} %vel_far.1, f32[6,4,16,128]{3,2,1,0:T(8,128)} %green_far.1, ...), custom_call_target="tpu_custom_call" | custom-call | tf_op jit(solution)/shard_map/membrane_step/pallas_call | solution.py:1054
  23.6 1.1 %finish_step.1 = (f32[3,4,16,128]{3,2,1,0:T(8,128)}, f32[6,4,16,128]{3,2,1,0:T(8,128)}, f32[4,16,128]{2,1,0:T(8,128)}) custom-call(f32[3,4,16,128]{3,2,1,0:T(8,128)S(1)} %get-tuple-element.9.predicted, f32[6,4,16,128]{3,2,1,0:T(8,128)S(1)} %get-tuple-element.10.green, f32[4,16,128]{2,1,0:T(8,128)S(1)} %get-tuple-element.11.fraction, ...), custom_call_target="tpu_custom_call" | custom-call | tf_op jit(solution)/shard_map/finish_step/pallas_call | solution.py:1069
